TPU v7x, 32 devices: a whole 2x2x4 slice. The times are simulated.
32 devices in a mesh: ia: 2 (over y), ja: 4 (over x, core), ka: 4 (over z).
Axes of the slice: x: 2, y: 2, z: 4, core: 2. Of those that a mesh axis runs over, the one named last changes fastest.
Arguments:
- tensor: float32 [32, 256, 8192], P('ia', 'ka', 'ja'), may hold values from -6 to 6
- factor_b: float32 [8192, 64], P(('ja', 'ka')), may hold values from -1 to 1
- factor_c: float32 [256, 64], P('ka'), may hold values from -1 to 1
Outputs:
- factor_a: float32 [32, 64], P(('ia', 'ja', 'ka'))
- mode_two: float32 [64, 4, 2048], P(None, 'ja', ('ia', 'ka'))
All inputs are finite; a program needn't handle non-finite values.
Results may differ from a plain program's by a relative error of at most 0.00026.
Values sent between devices are 32-bit elements; how exact they have to be, the bound alone decides.
No kernel may reach another device: no remote copies, remote signals or barrier semaphores. Data moves between devices by JAX's collectives and lax.ppermute only.
A program may use at most 64 MiB of HBM per device.

v0:
```python
import jax
import jax.numpy as jnp
from jax import lax
from jax.sharding import PartitionSpec as P


def body(tensor, factor_b, factor_c):
    highest = lax.Precision.HIGHEST
    factor_rank = factor_c.shape[1]
    row_block = tensor.shape[0]
    column_block = tensor.shape[2]
    local_b = jnp.dot(factor_b.T, factor_b, precision=highest, preferred_element_type=jnp.float32)
    local_c = jnp.dot(factor_c.T, factor_c, precision=highest, preferred_element_type=jnp.float32)
    gram_b = lax.psum(local_b, ("ja", "ka"))
    gram_c = lax.psum(local_c, "ka")
    triangle = jnp.linalg.cholesky(gram_b * gram_c)
    partial_value = jnp.einsum("ikj,kr->rij", tensor, factor_c, precision=highest)
    mode_one = jnp.einsum(
        "rij,jr->ir",
        partial_value,
        lax.all_gather(factor_b, "ka", axis=0, tiled=True),
        precision=highest,
    )
    empty_two = jnp.zeros((factor_rank, column_block), jnp.float32)
    full_sum = lax.psum(mode_one, ("ja", "ka"))
    a_block = jax.scipy.linalg.cho_solve((triangle, True), full_sum.T).T
    row_count = row_block // (lax.axis_size("ja") * lax.axis_size("ka"))
    offset = (lax.axis_index("ja") * lax.axis_size("ka") + lax.axis_index("ka")) * row_count
    a_rows = lax.dynamic_slice_in_dim(a_block, offset, row_count, 0)
    contracted = jnp.einsum("ikj,kr->rij", tensor, factor_c, precision=highest)
    mode_partial = empty_two + jnp.einsum("rij,ir->rj", contracted, a_block, precision=highest)
    reduced = lax.psum_scatter(mode_partial, ("ia", "ka"), scatter_dimension=1, tiled=True)
    return (a_rows, reduced.reshape(factor_rank, 1, reduced.shape[1]))


def solution(mesh):
    placed = (P("ia", "ka", "ja"), P(("ja", "ka"), None), P("ka", None))
    return jax.shard_map(
        body,
        mesh=mesh,
        in_specs=placed,
        out_specs=(P(("ia", "ja", "ka"), None), P(None, "ja", ("ia", "ka"))),
        check_vma=False,
    )
```

profile of v0, /device:TPU:0, one launch (start us, length us, event | category | flops | bytes accessed | tf_op | source)
XLA Modules:
  0.0 229.5 jit_solution(2462762528005702529)
XLA Ops:
  7.2 0.0 copy-start
  7.2 0.0 reduce-scatter.2.cloned.1.call-start
  7.2 17.6 %all_gather.3 = f32[2048,64]{0,1:T(8,128)S(1)} all-gather(f32[512,64]{0,1:T(8,128)} %param.4), channel_id=1, replica_groups=mesh['ia'=2,'ja'=4,'ka'=4] {'ka'}, dimensions={0}, use_global_device_ids=true | all-gather | bytes 655360 | tf_op jit(solution)/shard_map/all_gather | solution.py:21
  24.8 1.2 fusion.13
  26.1 0.0 copy-done
  26.1 0.2 fusion.14
  26.3 11.6 %fusion.6 = f32[64,16,2048]{2,0,1:T(8,128)} fusion(f32[16,64,2048]{2,1,0:T(8,128)} %param.3, f32[64,64]{1,0:T(8,128)S(1)} %copy-done), kind=kOutput, calls=%fused_computation.8 | convolution fusion | flops 1610612736 | bytes 16793600 | tf_op jit(solution)/shard_map/ikj,kr->rij/dot_general | solution.py:17
  37.9 19.8 %psum.22 = f32[64,64]{0,1:T(8,128)S(1)} all-reduce(f32[64,64]{0,1:T(8,128)S(1)} %fusion.14), channel_id=1, replica_groups=mesh['ia'=2,'ja'=4,'ka'=4] {'ka'}, use_global_device_ids=true, to_apply=%region_1.0 | all-reduce | flops 4096 | bytes 32768 | tf_op jit(solution)/shard_map/psum | solution.py:15
  57.7 17.9 %fusion.2 = f32[64,1,16]{2,1,0:T(1,128)S(1)} fusion(f32[64,16,2048]{2,0,1:T(8,128)} %fusion.6, f32[2048,64,1]{0,1,2:T(8,128)S(1)} %bitcast.31), kind=kOutput, calls=%fused_computation.2 | convolution fusion | flops 25165824 | bytes 8916992 | tf_op jit(solution)/shard_map/rij,jr->ir/dot_general | solution.py:18
  75.6 58.2 %all-reduce = (f32[16,64]{0,1:T(8,128)S(1)}, f32[64,64]{0,1:T(8,128)S(1)}) all-reduce(f32[16,64]{0,1:T(8,128)S(1)} %bitcast.33, f32[64,64]{0,1:T(8,128)S(1)} %fusion.13), channel_id=1, replica_groups=mesh['ia'=2,'ja'=4,'ka'=4] {'ja','ka'}, use_global_device_ids=true, to_apply=%region_4.5 | all-reduce | flops 5120 | bytes 40960 | tf_op jit(solution)/shard_map/psum | solution.py:25
  133.8 0.1 copy.7
  133.9 5.8 %cholesky.16 = f32[64,64]{1,0:T(8,128)S(1)} custom-call(f32[64,64]{1,0:T(8,128)S(1)} %fusion.12), custom_call_target="Cholesky" | custom-call | tf_op jit(solution)/shard_map/jit(cholesky)/cholesky | solution.py:16
  139.7 0.6 compare_reduce_fusion
  140.4 0.7 fusion.5
  141.0 4.9 %custom-call.10 = f32[1,64,64]{1,2,0:T(8,128)S(1)} custom-call(f32[1,64,64]{2,1,0:T(8,128)S(1)} %fusion.5), custom_call_target="InvertDiagBlocksLowerTriangular" | custom-call | tf_op jit(solution)/shard_map/jit(_cho_solve)/triangular_solve | solution.py:26
  145.9 0.3 fusion.10
  146.2 0.2 fusion.8
  146.4 0.1 copy.15
  146.5 12.3 %fusion = f32[64,1,2048]{2,1,0:T(1,128)S(1)} fusion(f32[16,64,1]{0,2,1:T(1,128)S(1)} %copy.15, f32[64,16,2048]{2,0,1:T(8,128)} %fusion.6), kind=kOutput, calls=%fused_computation | convolution fusion | flops 25165824 | bytes 8916992 | tf_op jit(solution)/shard_map/rij,ir->rj/dot_general | solution.py:31
  158.8 1.0 copy.25
  159.8 0.0 reduce-scatter.2.cloned.1.call-update
  159.8 0.5 constant_dynamic-slice_fusion
  160.3 60.9 %reduce-scatter.2.cloned.1.call-done = f32[64,256]{1,0:T(8,128)} async-done(((f32[64,2048]{1,0:T(8,128)}), f32[64,256]{1,0:T(8,128)}) %reduce-scatter.2.cloned.1.call-update) | async-done | bytes 65552 | tf_op jit(solution)/shard_map/reduce_scatter | solution.py:32
  221.2 1.5 reshape.20
  (3 shorter events, 0.0 us)
Async XLA Ops:
  7.2 18.9 %copy-start = (f32[64,64]{1,0:T(8,128)S(1)}, f32[64,64]{1,0:T(8,128)}, u32[]{:S(2)}) copy-start(f32[64,64]{1,0:T(8,128)} %param.5) | copy-start | bytes 49156
  7.2 214.0 %reduce-scatter.2.cloned.1.call-start = ((), (), s32[]{:S(2)}) async-start(), calls=%async_computation.1 | async-start | bytes 589824 | tf_op jit(solution)/shard_map/reduce_scatter | solution.py:32
Sparse Core Ops, SparseCore 0:
  159.9 61.2 reduce-scatter.1
where the time goes:
time: 230 us
  blocking collectives  95.6 us (42%)
  waiting for transfers between devices  60.9 us (26%)
  matrix products  43.7 us (19%)
  between operations  14.1 us (6%)
  other arithmetic  12.1 us (5%)
  local copies, waits for them, and re-layouts  3.15 us (1%)
    reduce_scatter x1, waiting for transfers between devices, body(): lax.psum_scatter(mode_partial, ('ia', 'ka'), scatter_dimension=1, tiled=T...  60.9 us
    psum x1, blocking collectives, body(): full_sum = lax.psum(mode_one, ('ja', 'ka'))  58.2 us
    psum x1, blocking collectives, body(): gram_c = lax.psum(local_c, 'ka')  19.8 us
    dot_general x1, matrix products, body(): jnp.einsum('rij,jr->ir', partial_value, lax.all_gather(factor_b, 'ka', ax...  17.9 us
    all_gather x1, blocking collectives, body(): lax.all_gather(factor_b, 'ka', axis=0, tiled=True)  17.6 us
    dot_general x1, matrix products, body(): jnp.einsum('rij,ir->rj', contracted, a_block, precision=highest)  12.3 us
    dot_general x1, matrix products, body(): jnp.einsum('ikj,kr->rij', tensor, factor_c, precision=highest)  11.6 us
    another operation x3, other arithmetic, body(): triangle = jnp.linalg.cholesky(gram_b * gram_c)  6.52 us
  transfers between devices with their start and end apart: 1, of which 1 were waited for; matrix products, arithmetic and copies ran while one was open for 0% of the time, Pallas kernels for 0%

commit v1 on v0

--- a/solution.py
+++ b/solution.py
@@ -22,7 +22,8 @@
         precision=highest,
     )
     empty_two = jnp.zeros((factor_rank, column_block), jnp.float32)
-    full_sum = lax.psum(mode_one, ("ja", "ka"))
+    inner = lax.psum(mode_one, "ka")
+    full_sum = lax.psum(inner, "ja")
     a_block = jax.scipy.linalg.cho_solve((triangle, True), full_sum.T).T
     row_count = row_block // (lax.axis_size("ja") * lax.axis_size("ka"))
     offset = (lax.axis_index("ja") * lax.axis_size("ka") + lax.axis_index("ka")) * row_count

time: 230 us -> 240 us (1.043)
  blocking collectives: 95.6 us -> 105 us
    psum x2 -> x3, blocking collectives: 78 us -> 87 us  [the longest x1 59.9 us: body(): gram_b = lax.psum(local_b, ('ja', 'ka'))]
where the time goes in v1:
time: 240 us
  blocking collectives  105 us (44%)
  waiting for transfers between devices  62.2 us (26%)
  matrix products  43.7 us (18%)
  between operations  14.1 us (6%)
  other arithmetic  12.1 us (5%)
  local copies, waits for them, and re-layouts  3.15 us (1%)
    reduce_scatter x1, waiting for transfers between devices, body(): lax.psum_scatter(mode_partial, ('ia', 'ka'), scatter_dimension=1, tiled=T...  62.2 us
    psum x1, blocking collectives, body(): gram_b = lax.psum(local_b, ('ja', 'ka'))  59.9 us
    dot_general x1, matrix products, body(): jnp.einsum('rij,jr->ir', partial_value, lax.all_gather(factor_b, 'ka', ax...  17.9 us
    all_gather x1, blocking collectives, body(): lax.all_gather(factor_b, 'ka', axis=0, tiled=True)  17.6 us
    psum x1, blocking collectives, body(): inner = lax.psum(mode_one, 'ka')  16.8 us
    dot_general x1, matrix products, body(): jnp.einsum('rij,ir->rj', contracted, a_block, precision=highest)  12.3 us
    dot_general x1, matrix products, body(): jnp.einsum('ikj,kr->rij', tensor, factor_c, precision=highest)  11.6 us
    psum x1, blocking collectives, body(): full_sum = lax.psum(inner, 'ja')  10.3 us
  transfers between devices with their start and end apart: 1, of which 1 were waited for; matrix products, arithmetic and copies ran while one was open for 0% of the time, Pallas kernels for 0%

profile of v1, /device:TPU:0, one launch (start us, length us, event | category | flops | bytes accessed | tf_op | source)
XLA Modules:
  0.0 239.9 jit_solution(10543073811703003133)
XLA Ops:
  7.2 0.0 copy-start
  7.2 0.0 reduce-scatter.2.cloned.1.call-start
  7.2 17.6 %all_gather.3 = f32[2048,64]{0,1:T(8,128)S(1)} all-gather(f32[512,64]{0,1:T(8,128)} %param.4), channel_id=1, replica_groups=mesh['ia'=2,'ja'=4,'ka'=4] {'ka'}, dimensions={0}, use_global_device_ids=true | all-gather | bytes 655360 | tf_op jit(solution)/shard_map/all_gather | solution.py:21
  24.8 1.2 fusion.13
  26.1 0.2 fusion.14
  26.3 11.6 %fusion.6 = f32[64,16,2048]{2,0,1:T(8,128)} fusion(f32[16,64,2048]{2,1,0:T(8,128)} %param.3, f32[64,64]{1,0:T(8,128)S(1)} %copy-done), kind=kOutput, calls=%fused_computation.8 | convolution fusion | flops 1610612736 | bytes 16793600 | tf_op jit(solution)/shard_map/ikj,kr->rij/dot_general | solution.py:17
  37.9 59.9 %psum.28 = f32[64,64]{0,1:T(8,128)S(1)} all-reduce(f32[64,64]{0,1:T(8,128)S(1)} %fusion.13), channel_id=1, replica_groups=mesh['ia'=2,'ja'=4,'ka'=4] {'ja','ka'}, use_global_device_ids=true, to_apply=%region_0.0 | all-reduce | flops 4096 | bytes 32768 | tf_op jit(solution)/shard_map/psum | solution.py:14
  97.8 17.9 %fusion.2 = f32[64,1,16]{2,1,0:T(1,128)S(1)} fusion(f32[64,16,2048]{2,0,1:T(8,128)} %fusion.6, f32[2048,64,1]{0,1,2:T(8,128)S(1)} %bitcast.31), kind=kOutput, calls=%fused_computation.2 | convolution fusion | flops 25165824 | bytes 8916992 | tf_op jit(solution)/shard_map/rij,jr->ir/dot_general | solution.py:18
  115.7 16.8 %all-reduce = (f32[16,64]{0,1:T(8,128)S(1)}, f32[64,64]{0,1:T(8,128)S(1)}) all-reduce(f32[16,64]{0,1:T(8,128)S(1)} %bitcast.33, f32[64,64]{0,1:T(8,128)S(1)} %fusion.14), channel_id=1, replica_groups=mesh['ia'=2,'ja'=4,'ka'=4] {'ka'}, use_global_device_ids=true, to_apply=%region_4.5 | all-reduce | flops 5120 | bytes 40960 | tf_op jit(solution)/shard_map/psum | solution.py:25
  132.5 0.1 copy.7
  132.6 5.8 %cholesky.16 = f32[64,64]{1,0:T(8,128)S(1)} custom-call(f32[64,64]{1,0:T(8,128)S(1)} %fusion.12), custom_call_target="Cholesky" | custom-call | tf_op jit(solution)/shard_map/jit(cholesky)/cholesky | solution.py:16
  138.5 0.6 compare_reduce_fusion
  139.1 0.7 fusion.5
  139.8 4.9 %custom-call.10 = f32[1,64,64]{1,2,0:T(8,128)S(1)} custom-call(f32[1,64,64]{2,1,0:T(8,128)S(1)} %fusion.5), custom_call_target="InvertDiagBlocksLowerTriangular" | custom-call | tf_op jit(solution)/shard_map/jit(_cho_solve)/triangular_solve | solution.py:27
  144.7 10.3 %psum.31 = f32[16,64]{0,1:T(8,128)S(1)} all-reduce(f32[16,64]{0,1:T(8,128)S(1)} %get-tuple-element.2), channel_id=1, replica_groups=mesh['ia'=2,'ja'=4,'ka'=4] {'ja'}, use_global_device_ids=true, to_apply=%region_5.6 | all-reduce | flops 1024 | bytes 8192 | tf_op jit(solution)/shard_map/psum | solution.py:26
  154.9 0.2 fusion.10
  155.2 0.2 fusion.8
  155.4 0.1 copy.15
  155.5 12.3 %fusion = f32[64,1,2048]{2,1,0:T(1,128)S(1)} fusion(f32[16,64,1]{0,2,1:T(1,128)S(1)} %copy.15, f32[64,16,2048]{2,0,1:T(8,128)} %fusion.6), kind=kOutput, calls=%fused_computation | convolution fusion | flops 25165824 | bytes 8916992 | tf_op jit(solution)/shard_map/rij,ir->rj/dot_general | solution.py:32
  167.8 1.0 copy.25
  168.8 0.0 reduce-scatter.2.cloned.1.call-update
  168.8 0.5 constant_dynamic-slice_fusion
  169.3 62.2 %reduce-scatter.2.cloned.1.call-done = f32[64,256]{1,0:T(8,128)} async-done(((f32[64,2048]{1,0:T(8,128)}), f32[64,256]{1,0:T(8,128)}) %reduce-scatter.2.cloned.1.call-update) | async-done | bytes 65552 | tf_op jit(solution)/shard_map/reduce_scatter | solution.py:33
  231.5 1.5 reshape.20
  (4 shorter events, 0.0 us)
Async XLA Ops:
  7.2 18.9 %copy-start = (f32[64,64]{1,0:T(8,128)S(1)}, f32[64,64]{1,0:T(8,128)}, u32[]{:S(2)}) copy-start(f32[64,64]{1,0:T(8,128)} %param.5) | copy-start | bytes 49156
  7.2 224.4 %reduce-scatter.2.cloned.1.call-start = ((), (), s32[]{:S(2)}) async-start(), calls=%async_computation.1 | async-start | bytes 589824 | tf_op jit(solution)/shard_map/reduce_scatter | solution.py:33
Sparse Core Ops, SparseCore 0:
  168.9 62.5 reduce-scatter.1
